TPU v7x, 32 devices: a whole 2x2x4 slice. The times are simulated.
32 devices in a mesh: space: 8 (over z, x), lag: 4 (over y, core).
Axes of the slice: x: 2, y: 2, z: 4, core: 2. Of those that a mesh axis runs over, the one named last changes fastest.
Arguments:
- prior: bfloat16 [8, 4, 64, 1024], P('lag', None, None, 'space'), may hold values from -6 to 6
- obs_value: float32 [8192], P('space'), may hold values from -6 to 6
- obs_weight: float32 [8192], P('space'), may hold values from 0.5 to 4
- obs_coef: float32 [4, 8192], P(None, 'space'), may hold values from 0.1 to 1
- obs_column: int32 [8192], P('space'), may hold values from 0 to 127
- obs_count: int32 [8], P('space'), may hold values from 512 to 1024
- halo_lists: int32 [2, 4096], P(None, 'space'), may hold values from 0 to 1023
- neighbours: int32 [64, 1024], P(None, 'space'), may hold values from 0 to 2047
- localization: float32 [64, 1024], P(None, 'space'), may hold values from 0.05 to 1
Outputs:
- analysis: bfloat16 [8, 4, 64, 1024], P('lag', None, None, 'space')
Inputs may be any that keep to these rules, and one draw needn't show every extreme that they name: `obs_column`: each observation's column within its own tile. `obs_count`: slots at or beyond a tile's count hold no observation. `halo_lists`: slot numbers within the sending tile. `neighbours`: positions in the extended list of the column's tile.
All inputs are finite; a program needn't handle non-finite values.
Results may differ from a plain program's by a relative error of at most 0.0062.
Values may be sent and summed in bfloat16 or wider, within the bound.
A program may use at most 64 MiB of HBM per device.

v0:
```python
import jax
import jax.numpy as jnp
from jax import lax
from jax.sharding import PartitionSpec as P

NSI = 2


def spread(block, axis, holder):
    block = jnp.where(lax.axis_index(axis) == holder, block, jnp.zeros_like(block))
    return lax.psum(block, axis)


def from_behind(value, axis, by):
    length = lax.axis_size(axis)
    pairs = [(i, i + by) for i in range(length) if 0 <= i + by < length]
    return lax.ppermute(value, axis, pairs)


def matmul(left, right):
    return jnp.einsum("ikc,kjc->ijc", left, right, precision=lax.Precision.HIGHEST)


def observe(newest, coef, column, value, weight, count):
    picked = jnp.take(newest, column, axis=2).astype(jnp.float32)
    hx = jnp.sum(coef[:, None, :] * picked, axis=0)
    mean_hx = jnp.mean(hx, axis=0)
    valid = (jnp.arange(column.shape[0]) < count).astype(jnp.float32)
    pert = ((hx - mean_hx[None, :]) * valid[None, :]).astype(jnp.bfloat16)
    info = jnp.stack([weight * valid, (value - mean_hx) * valid]).astype(jnp.bfloat16)
    return (pert, info)


def solve(ext_pert, ext_info, table, local_weight):
    members = ext_pert.shape[0]
    gathered = jnp.take(ext_pert, table, axis=1)
    ginfo = jnp.take(ext_info, table, axis=1)
    weighted = (
        gathered.astype(jnp.float32) * (local_weight * ginfo[0].astype(jnp.float32))[None]
    ).astype(jnp.bfloat16)
    gram = jnp.einsum("inc,jnc->ijc", gathered, weighted, preferred_element_type=jnp.float32)
    drive = jnp.einsum("inc,nc->ic", weighted, ginfo[1], preferred_element_type=jnp.float32)
    eye = jnp.eye(members, dtype=jnp.float32)[:, :, None]
    matrix = eye + gram / (members - 1)
    scale = jnp.sqrt(jnp.sum(matrix * matrix, axis=(0, 1)))
    ycur = matrix / scale[None, None, :]
    zcur = jnp.broadcast_to(eye, matrix.shape)
    for step in range(NSI):
        smat = 1.5 * eye - 0.5 * matmul(zcur, ycur)
        ycur = matmul(ycur, smat)
        zcur = matmul(smat, zcur)
    inverse = matmul(zcur, zcur) / scale[None, None, :]
    mean_weight = jnp.einsum("ijc,jc->ic", inverse, drive, precision=lax.Precision.HIGHEST) / (
        members - 1
    )
    root = zcur / jnp.sqrt(scale)[None, None, :]
    return (root + mean_weight[:, None, :]).astype(jnp.bfloat16)


def body(
    prior,
    obs_value,
    obs_weight,
    obs_coef,
    obs_column,
    obs_count,
    halo_lists,
    neighbours,
    localization,
):
    lags = lax.axis_size("lag")
    newest = spread(prior[-1], "lag", lags - 1)
    pert, info = observe(newest, obs_coef, obs_column, obs_value, obs_weight, obs_count[0])
    upward = (jnp.take(pert, halo_lists[0], axis=1), jnp.take(info, halo_lists[0], axis=1))
    downward = (jnp.take(pert, halo_lists[1], axis=1), jnp.take(info, halo_lists[1], axis=1))
    below_pert, below_info = from_behind((upward[0], upward[1]), "space", 1)
    above_pert, above_info = from_behind((downward[0], downward[1]), "space", -1)
    ext_pert = jnp.concatenate([pert, below_pert, above_pert], axis=1)
    ext_info = jnp.concatenate([info, below_info, above_info], axis=1)
    share = neighbours.shape[1] // lags
    start = lax.axis_index("lag") * share
    table = lax.dynamic_slice_in_dim(neighbours, start, share, 1)
    local_weight = lax.dynamic_slice_in_dim(localization, start, share, 1)
    portion = solve(ext_pert, ext_info, table, local_weight)
    trans = lax.all_gather(portion, "lag", axis=2, tiled=True)
    values = prior.astype(jnp.float32)
    prior_mean = jnp.mean(values, axis=2, keepdims=True)
    prior_pert = (values - prior_mean).astype(jnp.bfloat16)
    mixed = jnp.einsum("lskc,kjc->lsjc", prior_pert, trans, preferred_element_type=jnp.float32)
    return (prior_mean + mixed).astype(jnp.bfloat16)


def solution(mesh):
    return jax.shard_map(
        body,
        mesh=mesh,
        in_specs=(
            P("lag", None, None, "space"),
            P("space"),
            P("space"),
            P(None, "space"),
            P("space"),
            P("space"),
            P(None, "space"),
            P(None, "space"),
            P(None, "space"),
        ),
        out_specs=P("lag", None, None, "space"),
        check_vma=False,
    )
```

profile of v0, /device:TPU:0, one launch (start us, length us, event | category | flops | bytes accessed | tf_op | source)
XLA Modules:
  0.0 141.3 jit_solution(15085196720965544644)
XLA Ops:
  12.9 0.9 copy.73
  13.9 30.3 %all-reduce.2.cloned.1.call-done = bf16[4,64,128]{1,0,2:T(4,128)(2,1)} async-done(((bf16[4,64,128]{1,0,2:T(4,128)(2,1)}), bf16[4,64,128]{1,0,2:T(4,128)(2,1)}) %all-reduce.2.cloned.1.call-update) | async-done | bytes 65552 | tf_op jit(solution)/shard_map/psum | solution.py:11
  44.2 4.5 %gather_fusion = bf16[1024,4,64]{2,1,0:T(4,128)(2,1)S(1)} fusion(bf16[4,64,128]{1,0,2:T(4,128)(2,1)} %all-reduce.2.cloned.1.call-done, s32[1024]{0:T(1024)S(1)} %fusion.24), kind=kCustom, calls=%fused_computation.4 | custom fusion | bytes 1052672 | tf_op jit(solution)/shard_map/jit(_take)/gather | solution.py:25
  48.7 16.1 %fusion.3 = (f32[64,1024]{0,1:T(8,128)S(1)}, f32[1024]{0:T(1024)S(1)}) fusion(f32[4,1024]{0,1:T(8,128)S(1)} %copy.73, bf16[1024,4,64]{2,1,0:T(4,128)(2,1)S(1)} %gather_fusion, pred[1024]{0:T(1024)(128)(4,1)S(1)} %compare_and_fusion.1), kind=kLoop, calls=%fused_computation.11 | loop fusion | flops 1244160 | bytes 807936 | tf_op jit(solution)/shard_map/reduce_sum | solution.py:26
  65.2 1.3 gather_fusion.4
  66.5 1.3 gather_fusion.3
  68.1 1.3 gather_fusion.6
  69.5 1.3 gather_fusion.5
  71.2 3.4 %collective-permute-start.2 = (bf16[2,512]{0,1:T(8,128)(2,1)S(1)}, bf16[2,512]{0,1:T(8,128)(2,1)S(1)}, u32[]{:S(2)}, u32[]{:S(2)}) collective-permute-start(bf16[2,512]{0,1:T(8,128)(2,1)S(1)} %select_bitcast_fusion.1), channel_id=1, source_target_pairs={{0,4},{4,8},{8,12},{12,16},{16,20},{20,24},{24,28},{1,5},{5,9},{9,... | collective-permute-start | bytes 6152 | tf_op jit(solution)/shard_map/ppermute | solution.py:17
  74.6 1.3 collective-permute-start.3
  76.1 4.6 %collective-permute-start = (bf16[64,512]{0,1:T(8,128)(2,1)S(1)}, bf16[64,512]{0,1:T(8,128)(2,1)S(1)}, u32[]{:S(2)}, u32[]{:S(2)}) collective-permute-start(bf16[64,512]{0,1:T(8,128)(2,1)S(1)} %select_bitcast_fusion.3), channel_id=1, source_target_pairs={{0,4},{4,8},{8,12},{12,16},{16,20},{20,24},{24,28},{1,5},{5,9},{9,... | collective-permute-start | bytes 196616 | tf_op jit(solution)/shard_map/ppermute | solution.py:17
  80.6 1.5 %collective-permute-start.1 = (bf16[64,512]{0,1:T(8,128)(2,1)S(1)}, bf16[64,512]{0,1:T(8,128)(2,1)S(1)}, u32[]{:S(2)}, u32[]{:S(2)}) collective-permute-start(bf16[64,512]{0,1:T(8,128)(2,1)S(1)} %select_bitcast_fusion.2), channel_id=1, source_target_pairs={{4,0},{8,4},{12,8},{16,12},{20,16},{24,20},{28,24},{5,1},{9,5},{13... | collective-permute-start | bytes 196616 | tf_op jit(solution)/shard_map/ppermute | solution.py:17
  82.2 6.2 %gather_fusion.2 = bf16[2048,2]{1,0:T(8,128)(2,1)S(1)} fusion(bf16[2,2048]{0,1:T(8,128)(2,1)S(1)} %pad_maximum_fusion.1, s32[2048]{0:T(1024)S(1)} %broadcast_clamp_fusion), kind=kCustom, calls=%fused_computation.6 | custom fusion | bytes 24576 | tf_op jit(solution)/shard_map/jit(_take)/gather | solution.py:37
  89.3 6.2 %gather_fusion.1 = bf16[2048,64]{1,0:T(8,128)(2,1)S(1)} fusion(bf16[64,2048]{0,1:T(8,128)(2,1)S(1)} %pad_maximum_fusion, s32[2048]{0:T(1024)S(1)} %broadcast_clamp_fusion), kind=kCustom, calls=%fused_computation.5 | custom fusion | bytes 532480 | tf_op jit(solution)/shard_map/jit(_take)/gather | solution.py:36
  96.7 1.2 fusion.8
  97.9 1.2 convolution_bitcast_fusion.1
  99.1 1.0 convolution_bitcast_fusion.2
  100.5 1.3 fusion.6
  101.8 1.2 convolution_bitcast_fusion
  103.0 1.2 fusion.4
  104.2 1.0 fusion.28
  105.5 1.0 copy.87
  106.8 24.5 %all-gather.2.cloned.1.call-done = bf16[64,64,128]{1,0,2:T(8,128)(2,1)} async-done(((bf16[64,64,32]{1,0,2:T(8,128)(2,1)}), bf16[64,64,128]{1,0,2:T(8,128)(2,1)}) %all-gather.2.cloned.1.call-update) | async-done | bytes 1048592 | tf_op jit(solution)/shard_map/all_gather | solution.py:85
  131.3 2.2 %fusion = f32[128,64,2,4]{1,3,2,0:T(4,128)S(1)} fusion(bf16[2,4,64,128]{2,1,0,3:T(4,128)(2,1)S(1)} %copy.88, bf16[64,64,128]{1,0,2:T(8,128)(2,1)} %all-gather.2.cloned.1.call-done), kind=kOutput, calls=%fused_computation.7 | convolution fusion | flops 8388608 | bytes 1441792 | tf_op jit(solution)/shard_map/lskc,kjc->lsjc/dot_general | solution.py:89
  (64 shorter events, 10.8 us)
Async XLA Ops:
  6.5 37.7 %all-reduce.2.cloned.1.call-start = ((), (), s32[]{:S(2)}) async-start(), calls=%async_computation | async-start | bytes 262144 | tf_op jit(solution)/shard_map/psum | solution.py:11
  8.2 56.6 %copy-start.2 = (f32[1024]{0:T(1024)S(1)}, f32[1024]{0:T(1024)}, u32[]{:S(2)}) copy-start(f32[1024]{0:T(1024)} %param.14) | copy-start | bytes 12292
  8.3 123.0 %all-gather.2.cloned.1.call-start = ((), (), s32[]{:S(2)}) async-start(), calls=%async_computation.1 | async-start | bytes 2621440 | tf_op jit(solution)/shard_map/all_gather | solution.py:85
  66.5 22.4 %copy-start.1 = (f32[64,128]{1,0:T(8,128)S(1)}, f32[64,128]{1,0:T(8,128)}, u32[]{:S(2)}) copy-start(f32[64,128]{1,0:T(8,128)} %param.21) | copy-start | bytes 98308
  71.2 10.9 %collective-permute-start.2 = (bf16[2,512]{0,1:T(8,128)(2,1)S(1)}, bf16[2,512]{0,1:T(8,128)(2,1)S(1)}, u32[]{:S(2)}, u32[]{:S(2)}) collective-permute-start(bf16[2,512]{0,1:T(8,128)(2,1)S(1)} %select_bitcast_fusion.1), channel_id=1, source_target_pairs={{0,4},{4,8},{8,12},{12,16},{16,20},{20,24},{24,28},{1,5},{5,9},{9,... | collective-permute-start | bytes 6152 | tf_op jit(solution)/shard_map/ppermute | solution.py:17
  74.6 7.5 %collective-permute-start.3 = (bf16[2,512]{0,1:T(8,128)(2,1)S(1)}, bf16[2,512]{0,1:T(8,128)(2,1)S(1)}, u32[]{:S(2)}, u32[]{:S(2)}) collective-permute-start(bf16[2,512]{0,1:T(8,128)(2,1)S(1)} %select_bitcast_fusion), channel_id=1, source_target_pairs={{4,0},{8,4},{12,8},{16,12},{20,16},{24,20},{28,24},{5,1},{9,5},{13... | collective-permute-start | bytes 6152 | tf_op jit(solution)/shard_map/ppermute | solution.py:17
  76.1 13.1 %collective-permute-start = (bf16[64,512]{0,1:T(8,128)(2,1)S(1)}, bf16[64,512]{0,1:T(8,128)(2,1)S(1)}, u32[]{:S(2)}, u32[]{:S(2)}) collective-permute-start(bf16[64,512]{0,1:T(8,128)(2,1)S(1)} %select_bitcast_fusion.3), channel_id=1, source_target_pairs={{0,4},{4,8},{8,12},{12,16},{16,20},{20,24},{24,28},{1,5},{5,9},{9,... | collective-permute-start | bytes 196616 | tf_op jit(solution)/shard_map/ppermute | solution.py:17
  80.6 8.6 %collective-permute-start.1 = (bf16[64,512]{0,1:T(8,128)(2,1)S(1)}, bf16[64,512]{0,1:T(8,128)(2,1)S(1)}, u32[]{:S(2)}, u32[]{:S(2)}) collective-permute-start(bf16[64,512]{0,1:T(8,128)(2,1)S(1)} %select_bitcast_fusion.2), channel_id=1, source_target_pairs={{4,0},{8,4},{12,8},{16,12},{20,16},{24,20},{28,24},{5,1},{9,5},{13... | collective-permute-start | bytes 196616 | tf_op jit(solution)/shard_map/ppermute | solution.py:17
  104.2 2.3 %copy-start = (bf16[2,4,64,128]{3,2,1,0:T(8,128)(2,1)S(1)}, bf16[2,4,64,128]{3,2,1,0:T(8,128)(2,1)}, u32[]{:S(2)}) copy-start(bf16[2,4,64,128]{3,2,1,0:T(8,128)(2,1)} %param.13) | copy-start | bytes 393220
Sparse Core Ops, SparseCore 0:
  9.6 34.4 all-reduce.1
  106.6 24.6 all-gather.1
where the time goes:
time: 142 us; the launch traced here: 141 us
  waiting for transfers between devices  54.8 us (39%)
  local copies, waits for them, and re-layouts  28 us (20%)
  other arithmetic  22.1 us (16%)
  between operations  14.5 us (10%)
  matrix products  11.2 us (8%)
  starting transfers between devices  10.7 us (8%)
    psum x1, waiting for transfers between devices, spread(): return lax.psum(block, axis)  30.3 us
    all_gather x1, waiting for transfers between devices, body(): trans = lax.all_gather(portion, 'lag', axis=2, tiled=True)  24.5 us
    reduce_sum x1, other arithmetic, observe(): hx = jnp.sum(coef[:, None, :] * picked, axis=0)  16.1 us
    ppermute x4, starting transfers between devices, from_behind(): return lax.ppermute(value, axis, pairs)  10.7 us
    dot_general x6, matrix products, matmul(): jnp.einsum('ikc,kjc->ijc', left, right, precision=lax.Precision.HIGHEST)  7.1 us
    gather x2, local copies, waits for them, and re-layouts, solve(): gathered = jnp.take(ext_pert, table, axis=1)  6.79 us
    gather x2, local copies, waits for them, and re-layouts, solve(): ginfo = jnp.take(ext_info, table, axis=1)  6.67 us
    gather x1, local copies, waits for them, and re-layouts, observe(): picked = jnp.take(newest, column, axis=2).astype(jnp.float32)  4.46 us
  transfers between devices with their start and end apart: 6, of which 2 were waited for; matrix products, arithmetic and copies ran while one was open for 9% of the time, Pallas kernels for 0%

commit v1 on v0

v1 whole, which is shorter than its diff:
```python
import functools

import jax
import jax.numpy as jnp
from jax import lax
from jax.experimental import pallas as pl
from jax.experimental.pallas import tpu as pltpu
from jax.sharding import PartitionSpec as P

MESH = pl.DeviceIdType.MESH
F32 = jnp.float32
BF16 = jnp.bfloat16
PACK = 4
VMEM = pl.BlockSpec(memory_space=pltpu.VMEM)
ANY = pl.BlockSpec(memory_space=pl.ANY)
SMEM = pl.BlockSpec(memory_space=pltpu.SMEM)


def iota(shape, dim):
    return lax.broadcasted_iota(jnp.int32, shape, dim)


def onehot(row, depth):
    return jnp.where(row == iota((depth, row.shape[1]), 0), 1.0, 0.0).astype(BF16)


def dot(a, b):
    return jnp.dot(a, b, preferred_element_type=F32)


def split(x):
    high = x.astype(BF16)
    return high, (x - high.astype(F32)).astype(BF16)


def columns_kernel(prior_ref, send_ref, turned):
    windows, species, members, cols = prior_ref.shape
    rows = windows * species
    for r in range(rows):
        x = prior_ref[r // species, r % species].astype(F32)
        turned[r * cols : (r + 1) * cols, :] = jnp.concatenate([x, x], axis=0).T
    low = iota((rows, 2 * members), 1) < members
    share = cols // send_ref.shape[0]
    for c in range(0, cols, 2):
        even = turned[pl.ds(c, rows, stride=cols), :]
        odd = turned[pl.ds(c + 1, rows, stride=cols), :]
        at = (c % share) * members
        send_ref[c // share, :, at : at + 2 * members] = jnp.where(low, even, odd).astype(BF16)


def restore_kernel(got_ref, out_ref, turned):
    windows, species, members, cols = out_ref.shape
    rows = windows * species
    share = cols // got_ref.shape[0]
    for c in range(0, cols, 2):
        at = (c % share) * members
        x = got_ref[c // share, :, at : at + 2 * members].astype(F32)
        turned[pl.ds(c, rows, stride=cols), :] = x
        turned[pl.ds(c + 1, rows, stride=cols), :] = pltpu.roll(x, members, 1)
    for r in range(rows):
        x = turned[r * cols : (r + 1) * cols, :].T
        out_ref[r // species, r % species] = x[:members].astype(BF16)


def greet_lag(lags, me):
    barrier = pltpu.get_barrier_semaphore()
    for d in range(1, lags):
        pl.semaphore_signal(barrier, inc=1, device_id={"lag": lax.rem(me + d, lags)}, device_id_type=MESH)
    pl.semaphore_wait(barrier, lags - 1)


def swap(lags, me, send_ref, got_ref, send_sem, recv_sem):
    copies = []
    for d in range(1, lags):
        peer = lax.rem(me + d, lags)
        copies.append(
            pltpu.make_async_remote_copy(
                src_ref=send_ref.at[peer],
                dst_ref=got_ref.at[me],
                send_sem=send_sem.at[d - 1],
                recv_sem=recv_sem.at[d - 1],
                device_id={"lag": peer},
                device_id_type=MESH,
            )
        )
    return copies


def open_kernel(lags, prior_ref, send_ref, newest_ref, got_ref, ssem, rsem, nssem, nrsem, lsem):
    me = lax.axis_index("lag")
    holder = lags - 1
    last = prior_ref.shape[0] - 1
    greet_lag(lags, me)

    def spread(d):
        return pltpu.make_async_remote_copy(
            src_ref=prior_ref.at[last],
            dst_ref=newest_ref,
            send_sem=nssem.at[d],
            recv_sem=nrsem,
            device_id={"lag": lax.rem(me + d + 1, lags)},
            device_id_type=MESH,
        )

    mine = pltpu.make_async_copy(send_ref.at[me], got_ref.at[me], lsem.at[0])
    own = pltpu.make_async_copy(prior_ref.at[last], newest_ref, lsem.at[1])

    @pl.when(me == holder)
    def _():
        for d in range(lags - 1):
            spread(d).start()
        own.start()

    mine.start()
    copies = swap(lags, me, send_ref, got_ref, ssem, rsem)
    for copy in copies:
        copy.start()
    for copy in copies:
        copy.wait()
    mine.wait()

    @pl.when(me == holder)
    def _():
        for d in range(lags - 1):
            spread(d).wait_send()
        own.wait()

    @pl.when(me != holder)
    def _():
        spread(0).wait_recv()


def close_kernel(lags, send_ref, got_ref, ssem, rsem, lsem):
    me = lax.axis_index("lag")
    greet_lag(lags, me)
    mine = pltpu.make_async_copy(send_ref.at[me], got_ref.at[me], lsem)
    copies = swap(lags, me, send_ref, got_ref, ssem, rsem)
    for copy in copies:
        copy.start()
    mine.start()
    for copy in copies:
        copy.wait()
    mine.wait()


def observe_kernel(newest_ref, coef_ref, column_ref, value_ref, weight_ref, count_ref, lists_ref, feat_ref, halo_ref):
    species, members, cols = newest_ref.shape
    slots = column_ref.shape[1]
    pick = onehot(column_ref[...], cols)
    hx = coef_ref[0:1, :] * dot(newest_ref[0], pick)
    for s in range(1, species):
        hx = hx + coef_ref[s : s + 1, :] * dot(newest_ref[s], pick)
    mean = jnp.sum(hx, axis=0, keepdims=True) / members
    valid = jnp.where(iota((1, slots), 1) < count_ref[0], 1.0, 0.0)
    feat_ref[:members] = ((hx - mean) * valid).astype(BF16)
    extra = feat_ref.shape[0] - members
    row = iota((extra, slots), 0)
    info0 = weight_ref[...] * valid
    info1 = (value_ref[...] - mean) * valid
    feat_ref[members:] = jnp.where(row == 0, info0, jnp.where(row == 1, info1, 0.0)).astype(BF16)
    feat = feat_ref[...]
    for r in range(2):
        halo_ref[r] = dot(feat, onehot(lists_ref[r : r + 1, :], slots)).astype(BF16)


def halo_kernel(tiles, halo_ref, got_ref, ssem, rsem):
    t = lax.axis_index("space")
    barrier = pltpu.get_barrier_semaphore()
    below, above = t > 0, t < tiles - 1
    up, down = jnp.minimum(t + 1, tiles - 1), jnp.maximum(t - 1, 0)

    @pl.when(above)
    def _():
        pl.semaphore_signal(barrier, inc=1, device_id={"space": up}, device_id_type=MESH)

    @pl.when(below)
    def _():
        pl.semaphore_signal(barrier, inc=1, device_id={"space": down}, device_id_type=MESH)

    @pl.when(below & above)
    def _():
        pl.semaphore_wait(barrier, 2)

    @pl.when(below != above)
    def _():
        pl.semaphore_wait(barrier, 1)

    def move(r, to):
        return pltpu.make_async_remote_copy(
            src_ref=halo_ref.at[r],
            dst_ref=got_ref.at[r],
            send_sem=ssem.at[r],
            recv_sem=rsem.at[r],
            device_id={"space": to},
            device_id_type=MESH,
        )

    @pl.when(above)
    def _():
        move(0, up).start()

    @pl.when(below)
    def _():
        move(1, down).start()

    @pl.when(above)
    def _():
        move(0, up).wait_send()
        move(1, up).wait_recv()

    @pl.when(below)
    def _():
        move(1, down).wait_send()
        move(0, down).wait_recv()


def solve_kernel(tiles, lags, feat_ref, halo_ref, table_ref, local_ref, prior_ref, out_ref, ext, tabs, locs):
    t, me = lax.axis_index("space"), lax.axis_index("lag")
    near, cols = table_ref.shape
    rows = prior_ref.shape[1]
    slots, halo = feat_ref.shape[1], halo_ref.shape[2]
    share = cols // lags
    members = prior_ref.shape[2] // share
    groups = share // PACK
    wide = PACK * members
    depth = slots + 2 * halo

    ext[:, :slots] = feat_ref[...]
    ext[:, slots : slots + halo] = jnp.where(t > 0, halo_ref[0].astype(F32), 0.0).astype(BF16)
    ext[:, slots + halo :] = jnp.where(t < tiles - 1, halo_ref[1].astype(F32), 0.0).astype(BF16)
    x = table_ref[...].astype(F32)
    tabs[...] = jnp.concatenate([x, x], axis=0).T
    x = local_ref[...]
    locs[...] = jnp.concatenate([x, x], axis=0).T

    start = pl.multiple_of(me * share, share)
    low = iota((1, 2 * near), 1) < near

    def row_of(ref, q):
        parts = []
        for m in range(0, PACK, 2):
            c = start + q * PACK + m
            parts.append(jnp.where(low, ref[pl.ds(c, 1), :], ref[pl.ds(c + 1, 1), :]))
        return jnp.concatenate(parts, axis=1)

    lane = iota((members, wide), 1)
    masks = [jnp.where(lane // members == m, 1.0, 0.0).astype(BF16) for m in range(PACK)]
    ones = jnp.concatenate(masks, axis=0)
    eye = jnp.where(lane % members == iota((members, wide), 0), 1.0, 0.0)

    def diag(x):
        return jnp.concatenate([x * mask for mask in masks], axis=0)

    qs = range(groups)
    table = [row_of(tabs, q).astype(jnp.int32) for q in qs]
    local = [row_of(locs, q) for q in qs]
    source = ext[...]
    picked = [dot(source, onehot(table[q], depth)) for q in qs]
    gathered = [picked[q][:members] for q in qs]
    weighted = [(gathered[q] * (local[q] * picked[q][members : members + 1])).astype(BF16) for q in qs]
    gram = [
        lax.dot_general(
            gathered[q].astype(BF16), diag(weighted[q]), (((1,), (1,)), ((), ())), preferred_element_type=F32
        )
        for q in qs
    ]
    matrix = [eye + gram[q] / (members - 1) for q in qs]
    total = [jnp.sum(matrix[q] * matrix[q], axis=0, keepdims=True) for q in qs]

    def group_sum(x):
        high, low_part = split(x)
        mid, last = split(x - high.astype(F32))
        count = x.shape[0]
        y = dot(jnp.concatenate([high.astype(F32), mid.astype(F32), last.astype(F32)], axis=0).astype(BF16), ones)
        return y[:count] + y[count : 2 * count] + y[2 * count :]

    scale2 = group_sum(jnp.concatenate(total, axis=0))
    root = lax.rsqrt(scale2)
    inv = [root[q : q + 1] for q in qs]
    a = [matrix[q] * inv[q] for q in qs]
    ab = [a[q].astype(BF16) for q in qs]
    p = [dot(ab[q], diag(ab[q])) for q in qs]
    pb = [p[q].astype(BF16) for q in qs]
    z = [
        2.25 * eye
        - 2.4375 * a[q]
        + 1.6875 * p[q]
        + dot((0.0625 * p[q] - 0.5625 * a[q]).astype(BF16), diag(pb[q]))
        for q in qs
    ]
    zs = [jnp.concatenate(split(z[q]), axis=0) for q in qs]

    def apply(q, x):
        high, small = split(x)
        y = dot(zs[q], diag(high))
        return y[:members] + y[members:] + dot(zs[q][:members], diag(small))

    drive = []
    for q in qs:
        x = weighted[q].astype(F32) * picked[q][members + 1 : members + 2]
        y = dot(jnp.concatenate(split(x), axis=0), ones)
        drive.append(y[:members] + y[members:])
    u = [apply(q, drive[q]) for q in qs]
    mean_weight = [apply(q, u[q]) for q in qs]
    for q in qs:
        trans = (z[q] * jnp.sqrt(inv[q]) + mean_weight[q] * (inv[q] / (members - 1))).astype(BF16)
        prior = jnp.concatenate([prior_ref[l, :, q * wide : (q + 1) * wide].astype(F32) for l in range(lags)], axis=0)
        mean = dot(prior.astype(BF16), ones) / members
        mixed = mean + dot((prior - mean).astype(BF16), diag(trans))
        for l in range(lags):
            out_ref[l, :, q * wide : (q + 1) * wide] = mixed[l * rows : (l + 1) * rows].astype(BF16)


def body(prior, obs_value, obs_weight, obs_coef, obs_column, obs_count, halo_lists, neighbours, localization):
    lags, tiles = lax.axis_size("lag"), lax.axis_size("space")
    windows, species, members, cols = prior.shape
    slots, halo, near = obs_column.shape[0], halo_lists.shape[1], neighbours.shape[0]
    share = cols // lags
    rows = windows * species
    block = jax.ShapeDtypeStruct((lags, rows, share * members), BF16)
    feats = members + 16
    turned = pltpu.VMEM((rows * cols, 2 * members), F32)

    send = pl.pallas_call(
        columns_kernel, out_shape=block, in_specs=[VMEM], out_specs=VMEM, scratch_shapes=[turned], name="columns"
    )(prior)
    newest, windows_all = pl.pallas_call(
        functools.partial(open_kernel, lags),
        out_shape=(jax.ShapeDtypeStruct((species, members, cols), BF16), block),
        in_specs=[ANY, ANY],
        out_specs=(ANY, ANY),
        scratch_shapes=[
            pltpu.SemaphoreType.DMA((lags - 1,)),
            pltpu.SemaphoreType.DMA((lags - 1,)),
            pltpu.SemaphoreType.DMA((lags - 1,)),
            pltpu.SemaphoreType.DMA,
            pltpu.SemaphoreType.DMA((2,)),
        ],
        compiler_params=pltpu.CompilerParams(collective_id=0, has_side_effects=True),
        name="open",
    )(prior, send)
    feat, listed = pl.pallas_call(
        observe_kernel,
        out_shape=(jax.ShapeDtypeStruct((feats, slots), BF16), jax.ShapeDtypeStruct((2, feats, halo), BF16)),
        in_specs=[VMEM, VMEM, VMEM, VMEM, VMEM, SMEM, VMEM],
        out_specs=(VMEM, VMEM),
        name="observe",
    )(
        newest,
        obs_coef,
        obs_column.reshape(1, slots),
        obs_value.reshape(1, slots),
        obs_weight.reshape(1, slots),
        obs_count,
        halo_lists,
    )
    around = pl.pallas_call(
        functools.partial(halo_kernel, tiles),
        out_shape=jax.ShapeDtypeStruct((2, feats, halo), BF16),
        in_specs=[ANY],
        out_specs=ANY,
        scratch_shapes=[pltpu.SemaphoreType.DMA((2,)), pltpu.SemaphoreType.DMA((2,))],
        compiler_params=pltpu.CompilerParams(collective_id=1, has_side_effects=True),
        name="halo",
    )(listed)
    mixed = pl.pallas_call(
        functools.partial(solve_kernel, tiles, lags),
        out_shape=block,
        in_specs=[VMEM] * 5,
        out_specs=VMEM,
        scratch_shapes=[
            pltpu.VMEM((feats, slots + 2 * halo), BF16),
            pltpu.VMEM((cols, 2 * near), F32),
            pltpu.VMEM((cols, 2 * near), F32),
        ],
        name="solve",
    )(feat, around, neighbours, localization, windows_all)
    back = pl.pallas_call(
        functools.partial(close_kernel, lags),
        out_shape=block,
        in_specs=[ANY],
        out_specs=ANY,
        scratch_shapes=[
            pltpu.SemaphoreType.DMA((lags - 1,)),
            pltpu.SemaphoreType.DMA((lags - 1,)),
            pltpu.SemaphoreType.DMA,
        ],
        compiler_params=pltpu.CompilerParams(collective_id=2, has_side_effects=True),
        name="close",
    )(mixed)
    return pl.pallas_call(
        restore_kernel,
        out_shape=jax.ShapeDtypeStruct(prior.shape, BF16),
        in_specs=[VMEM],
        out_specs=VMEM,
        scratch_shapes=[turned],
        name="restore",
    )(back)


def solution(mesh):
    return jax.shard_map(
        body,
        mesh=mesh,
        in_specs=(
            P("lag", None, None, "space"),
            P("space"),
            P("space"),
            P(None, "space"),
            P("space"),
            P("space"),
            P(None, "space"),
            P(None, "space"),
            P(None, "space"),
        ),
        out_specs=P("lag", None, None, "space"),
        check_vma=False,
    )
```

time: 142 us -> 31.2 us (0.22)
  the two profiles are of different devices: /device:TPU:0 before, /device:TPU:17 now
where the time goes in v1:
time: 31.2 us; the launch traced here: 31 us
  Pallas kernels  30.3 us (97%)
  between operations  0.68 us (2%)
    pallas_call x1, Pallas kernels, body(): pl.pallas_call(functools.partial(halo_kernel, tiles), out_shape=jax.Shape...  7.4 us
    pallas_call x1, Pallas kernels, body(): pl.pallas_call(functools.partial(open_kernel, lags), out_shape=(jax.Shape...  6.21 us
    pallas_call x1, Pallas kernels, body(): pl.pallas_call(functools.partial(solve_kernel, tiles, lags), out_shape=bl...  5.8 us
    pallas_call x1, Pallas kernels, body(): pl.pallas_call(functools.partial(close_kernel, lags), out_shape=block, in...  4.55 us
    pallas_call x1, Pallas kernels, body(): pl.pallas_call(observe_kernel, out_shape=(jax.ShapeDtypeStruct((feats, sl...  2.39 us
    pallas_call x1, Pallas kernels, body(): pl.pallas_call(restore_kernel, out_shape=jax.ShapeDtypeStruct(prior.shape...  1.97 us
    pallas_call x1, Pallas kernels, body(): pl.pallas_call(columns_kernel, out_shape=block, in_specs=[VMEM], out_spec...  1.96 us

profile of v1, /device:TPU:17, one launch (start us, length us, event | category | flops | bytes accessed | tf_op | source)
XLA Modules:
  0.0 31.0 jit_solution(9963886325297963207)
XLA Ops:
  0.7 2.0 %columns.1.send_ref = bf16[4,8,2048]{2,1,0:T(8,128)(2,1)} custom-call(bf16[2,4,64,128]{3,2,1,0:T(8,128)(2,1)} %prior_ref.3), custom_call_target="tpu_custom_call" | custom-call | tf_op jit(solution)/shard_map/columns/pallas_call | solution.py:324
  2.6 6.2 %open.1 = (bf16[4,64,128]{2,1,0:T(8,128)(2,1)}, bf16[4,8,2048]{2,1,0:T(8,128)(2,1)}) custom-call(bf16[2,4,64,128]{3,2,1,0:T(8,128)(2,1)} %prior_ref.3, bf16[4,8,2048]{2,1,0:T(8,128)(2,1)} %columns.1.send_ref), custom_call_target="tpu_custom_call" | custom-call | tf_op jit(solution)/shard_map/open/pallas_call | solution.py:327
  8.8 2.4 %observe.1 = (bf16[80,1024]{1,0:T(8,128)(2,1)}, bf16[2,80,512]{2,1,0:T(8,128)(2,1)}) custom-call(bf16[4,64,128]{2,1,0:T(8,128)(2,1)} %get-tuple-element.9.newest_ref, f32[4,1024]{1,0:T(4,128)} %coef_ref.1, s32[1,1024]{1,0:T(1,128)} %bitcast.3, f32[1,1024]{1,0:T(1,128)} %bitcast.4, f32[1,1024]{1,0:T(1,128)} %bitcast.5, s32[1]{0:T(128)S(6)} %copy.10.count_ref, ...), custom_call_target="tpu_custom_call" | custom-call | tf_op jit(solution)/shard_map/observe/pallas_call | solution.py:342
  11.2 7.4 %halo.1.halo_ref = bf16[2,80,512]{2,1,0:T(8,128)(2,1)} custom-call(bf16[2,80,512]{2,1,0:T(8,128)(2,1)} %get-tuple-element.11.halo_ref), custom_call_target="tpu_custom_call" | custom-call | tf_op jit(solution)/shard_map/halo/pallas_call | solution.py:357
  18.6 5.8 %solve.1.send_ref = bf16[4,8,2048]{2,1,0:T(8,128)(2,1)} custom-call(bf16[80,1024]{1,0:T(8,128)(2,1)} %get-tuple-element.10.feat_ref, bf16[2,80,512]{2,1,0:T(8,128)(2,1)} %halo.1.halo_ref, s32[64,128]{1,0:T(8,128)} %table_ref.1, f32[64,128]{1,0:T(8,128)} %local_ref.1, bf16[4,8,2048]{2,1,0:T(8,128)(2,1)} %get-tuple-element.12.prior_ref), custom_call_target="tpu_custom_call" | custom-call | tf_op jit(solution)/shard_map/solve/pallas_call | solution.py:366
  24.4 4.6 %close.1.got_ref = bf16[4,8,2048]{2,1,0:T(8,128)(2,1)} custom-call(bf16[4,8,2048]{2,1,0:T(8,128)(2,1)} %solve.1.send_ref), custom_call_target="tpu_custom_call" | custom-call | tf_op jit(solution)/shard_map/close/pallas_call | solution.py:378
  29.0 2.0 %restore.1 = bf16[2,4,64,128]{3,2,1,0:T(8,128)(2,1)} custom-call(bf16[4,8,2048]{2,1,0:T(8,128)(2,1)} %close.1.got_ref), custom_call_target="tpu_custom_call" | custom-call | tf_op jit(solution)/shard_map/restore/pallas_call | solution.py:391

commit v2 on v0

v2 whole, which is shorter than its diff:
```python
import functools

import jax
import jax.numpy as jnp
from jax import lax
from jax.experimental import pallas as pl
from jax.experimental.pallas import tpu as pltpu
from jax.sharding import PartitionSpec as P

MESH = pl.DeviceIdType.MESH
F32 = jnp.float32
BF16 = jnp.bfloat16
PACK = 4
VMEM = pl.BlockSpec(memory_space=pltpu.VMEM)
ANY = pl.BlockSpec(memory_space=pl.ANY)
SMEM = pl.BlockSpec(memory_space=pltpu.SMEM)


def iota(shape, dim):
    return lax.broadcasted_iota(jnp.int32, shape, dim)


def onehot(row, depth):
    return jnp.where(row == iota((depth, row.shape[1]), 0), 1.0, 0.0).astype(BF16)


def dot(a, b):
    return jnp.dot(a, b, preferred_element_type=F32)


def split(x):
    high = x.astype(BF16)
    return high, (x - high.astype(F32)).astype(BF16)


def remote(src, dst, send_sem, recv_sem, where):
    return pltpu.make_async_remote_copy(
        src_ref=src, dst_ref=dst, send_sem=send_sem, recv_sem=recv_sem, device_id=where, device_id_type=MESH
    )


def kernel(
    tiles,
    lags,
    count_ref,
    prior_ref,
    value_ref,
    weight_ref,
    coef_ref,
    column_ref,
    lists_ref,
    table_ref,
    local_ref,
    out_ref,
    prior_v,
    value_v,
    weight_v,
    coef_v,
    column_v,
    lists_v,
    table_v,
    local_v,
    newest,
    turned,
    send,
    got,
    back,
    home,
    feat_v,
    listed,
    around,
    pick_v,
    list_v,
    near_v,
    tabs,
    locs,
    in_sem,
    new_send,
    new_recv,
    swap_send,
    swap_recv,
    halo_send,
    halo_recv,
    back_send,
    back_recv,
    self_sem,
):
    t, me = lax.axis_index("space"), lax.axis_index("lag")
    windows, species, members, cols = prior_v.shape
    rows = windows * species
    share = cols // lags
    slots, halo = column_v.shape[1], lists_v.shape[1]
    near = table_v.shape[0]
    holder = lags - 1
    below, above = t > 0, t < tiles - 1
    up, down = jnp.minimum(t + 1, tiles - 1), jnp.maximum(t - 1, 0)
    peers = [lax.rem(me + d, lags) for d in range(1, lags)]

    barrier = pltpu.get_barrier_semaphore()
    for peer in peers:
        pl.semaphore_signal(barrier, inc=1, device_id={"lag": peer}, device_id_type=MESH)

    @pl.when(above)
    def _():
        pl.semaphore_signal(barrier, inc=1, device_id={"space": up}, device_id_type=MESH)

    @pl.when(below)
    def _():
        pl.semaphore_signal(barrier, inc=1, device_id={"space": down}, device_id_type=MESH)

    pairs = [
        (prior_ref, prior_v),
        (column_ref, column_v),
        (lists_ref, lists_v),
        (coef_ref, coef_v),
        (value_ref, value_v),
        (weight_ref, weight_v),
        (table_ref, table_v),
        (local_ref, local_v),
    ]
    loads = [pltpu.make_async_copy(src, dst, in_sem.at[i]) for i, (src, dst) in enumerate(pairs)]
    for load in loads:
        load.start()

    @pl.when(below & above)
    def _():
        pl.semaphore_wait(barrier, lags + 1)

    @pl.when(below != above)
    def _():
        pl.semaphore_wait(barrier, lags)

    def spread(d):
        return remote(prior_ref.at[windows - 1], newest, new_send.at[d], new_recv, {"lag": peers[d]})

    own = pltpu.make_async_copy(prior_ref.at[windows - 1], newest, self_sem.at[0])

    @pl.when(me == holder)
    def _():
        for d in range(lags - 1):
            spread(d).start()
        own.start()

    loads[0].wait()
    for r in range(rows):
        x = prior_v[r // species, r % species].astype(F32)
        turned[r * cols : (r + 1) * cols, :] = jnp.concatenate([x, x], axis=0).T
    low = iota((1, 2 * members), 1) < members
    for c in range(0, cols, 2):
        even = turned[pl.ds(c, rows, stride=cols), :]
        odd = turned[pl.ds(c + 1, rows, stride=cols), :]
        at = (c % share) * members
        send[c // share, :, at : at + 2 * members] = jnp.where(low, even, odd).astype(BF16)
    for load in loads[1:]:
        load.wait()
    pick_v[...] = onehot(column_v[...], cols)
    for r in range(2):
        list_v[r] = onehot(lists_v[r : r + 1, :], slots)

    @pl.when(me == holder)
    def _():
        own.wait()

    @pl.when(me != holder)
    def _():
        spread(0).wait_recv()

    pick = pick_v[...]
    hx = coef_v[0:1, :] * dot(newest[0], pick)
    for s in range(1, species):
        hx = hx + coef_v[s : s + 1, :] * dot(newest[s], pick)
    mean = jnp.sum(hx, axis=0, keepdims=True) / members
    valid = jnp.where(iota((1, slots), 1) < count_ref[0], 1.0, 0.0)
    feat_v[:members] = ((hx - mean) * valid).astype(BF16)
    extra = feat_v.shape[0] - members
    row = iota((extra, slots), 0)
    info0 = weight_v[...] * valid
    info1 = (value_v[...] - mean) * valid
    feat_v[members:] = jnp.where(row == 0, info0, jnp.where(row == 1, info1, 0.0)).astype(BF16)
    feat = feat_v[...]
    for r in range(2):
        listed[r] = dot(feat, list_v[r]).astype(BF16)

    def move(r, to):
        return remote(listed.at[r], around.at[r], halo_send.at[r], halo_recv.at[r], {"space": to})

    @pl.when(above)
    def _():
        move(0, up).start()

    @pl.when(below)
    def _():
        move(1, down).start()

    @pl.when(t == 0)
    def _():
        around[0] = jnp.zeros(around.shape[1:], BF16)

    @pl.when(t == tiles - 1)
    def _():
        around[1] = jnp.zeros(around.shape[1:], BF16)

    mine = pltpu.make_async_copy(send.at[me], got.at[me], self_sem.at[1])
    mine.start()
    swaps = [
        remote(send.at[peer], got.at[me], swap_send.at[d], swap_recv.at[d], {"lag": peer})
        for d, peer in enumerate(peers)
    ]
    for copy in swaps:
        copy.start()

    x = table_v[...].astype(F32)
    tabs[...] = jnp.concatenate([x, x], axis=0).T
    x = local_v[...]
    locs[...] = jnp.concatenate([x, x], axis=0).T
    start = pl.multiple_of(me * share, share)
    low = iota((1, 2 * near), 1) < near
    groups = share // PACK
    wide = PACK * members
    qs = range(groups)

    def row_of(ref, q):
        parts = []
        for m in range(0, PACK, 2):
            c = start + q * PACK + m
            parts.append(jnp.where(low, ref[pl.ds(c, 1), :], ref[pl.ds(c + 1, 1), :]))
        return jnp.concatenate(parts, axis=1)

    lane = iota((members, wide), 1)
    masks = [jnp.where(lane // members == m, 1.0, 0.0).astype(BF16) for m in range(PACK)]
    ones = jnp.concatenate(masks, axis=0)
    eye = jnp.where(lane % members == iota((members, wide), 0), 1.0, 0.0)

    def diag(x):
        return jnp.concatenate([x * mask for mask in masks], axis=0)

    local = [row_of(locs, q) for q in qs]
    inner = []
    for q in qs:
        table = row_of(tabs, q).astype(jnp.int32)
        inner.append(dot(feat, onehot(table, slots)))
        near_v[q] = onehot(table - slots, 2 * halo)

    @pl.when(above)
    def _():
        move(0, up).wait_send()
        move(1, up).wait_recv()

    @pl.when(below)
    def _():
        move(1, down).wait_send()
        move(0, down).wait_recv()

    picked = [
        inner[q] + dot(around[0], near_v[q, :halo]) + dot(around[1], near_v[q, halo:]) for q in qs
    ]
    gathered = [picked[q][:members] for q in qs]
    weighted = [(gathered[q] * (local[q] * picked[q][members : members + 1])).astype(BF16) for q in qs]
    gram = [
        lax.dot_general(
            gathered[q].astype(BF16), diag(weighted[q]), (((1,), (1,)), ((), ())), preferred_element_type=F32
        )
        for q in qs
    ]
    matrix = [eye + gram[q] / (members - 1) for q in qs]
    total = [jnp.sum(matrix[q] * matrix[q], axis=0, keepdims=True) for q in qs]

    def group_sum(x):
        high, _ = split(x)
        mid, last = split(x - high.astype(F32))
        count = x.shape[0]
        y = dot(jnp.concatenate([high.astype(F32), mid.astype(F32), last.astype(F32)], axis=0).astype(BF16), ones)
        return y[:count] + y[count : 2 * count] + y[2 * count :]

    root = lax.rsqrt(group_sum(jnp.concatenate(total, axis=0)))
    inv = [root[q : q + 1] for q in qs]
    a = [matrix[q] * inv[q] for q in qs]
    ab = [a[q].astype(BF16) for q in qs]
    p = [dot(ab[q], diag(ab[q])) for q in qs]
    z = [
        2.25 * eye
        - 2.4375 * a[q]
        + 1.6875 * p[q]
        + dot((0.0625 * p[q] - 0.5625 * a[q]).astype(BF16), diag(p[q].astype(BF16)))
        for q in qs
    ]
    zs = [jnp.concatenate(split(z[q]), axis=0) for q in qs]

    def apply(q, x):
        high, small = split(x)
        y = dot(zs[q], diag(high))
        return y[:members] + y[members:] + dot(zs[q][:members], diag(small))

    drive = []
    for q in qs:
        x = weighted[q].astype(F32) * picked[q][members + 1 : members + 2]
        y = dot(jnp.concatenate(split(x), axis=0), ones)
        drive.append(y[:members] + y[members:])
    u = [apply(q, drive[q]) for q in qs]
    mean_weight = [apply(q, u[q]) for q in qs]
    trans = [
        (z[q] * jnp.sqrt(inv[q]) + mean_weight[q] * (inv[q] / (members - 1))).astype(BF16) for q in qs
    ]

    for copy in swaps:
        copy.wait()
    mine.wait()
    for q in qs:
        prior = jnp.concatenate([got[l, :, q * wide : (q + 1) * wide].astype(F32) for l in range(lags)], axis=0)
        mean = dot(prior.astype(BF16), ones) / members
        mixed = mean + dot((prior - mean).astype(BF16), diag(trans[q]))
        for l in range(lags):
            back[l, :, q * wide : (q + 1) * wide] = mixed[l * rows : (l + 1) * rows].astype(BF16)
    returns = [
        remote(back.at[peer], home.at[me], back_send.at[d], back_recv.at[d], {"lag": peer})
        for d, peer in enumerate(peers)
    ]
    for copy in returns:
        copy.start()
    mine = pltpu.make_async_copy(back.at[me], home.at[me], self_sem.at[2])
    mine.start()

    @pl.when(me == holder)
    def _():
        for d in range(lags - 1):
            spread(d).wait_send()

    mine.wait()
    for copy in returns:
        copy.wait()
    for c in range(0, cols, 2):
        at = (c % share) * members
        x = home[c // share, :, at : at + 2 * members].astype(F32)
        turned[pl.ds(c, rows, stride=cols), :] = x
        turned[pl.ds(c + 1, rows, stride=cols), :] = pltpu.roll(x, members, 1)
    for r in range(rows):
        x = turned[r * cols : (r + 1) * cols, :].T
        out_ref[r // species, r % species] = x[:members].astype(BF16)


def body(prior, obs_value, obs_weight, obs_coef, obs_column, obs_count, halo_lists, neighbours, localization):
    lags, tiles = lax.axis_size("lag"), lax.axis_size("space")
    windows, species, members, cols = prior.shape
    slots, halo, near = obs_column.shape[0], halo_lists.shape[1], neighbours.shape[0]
    share = cols // lags
    rows = windows * species
    block = pltpu.VMEM((lags, rows, share * members), BF16)
    feats = members + 16
    args = (
        prior,
        obs_value.reshape(1, slots),
        obs_weight.reshape(1, slots),
        obs_coef,
        obs_column.reshape(1, slots),
        halo_lists,
        neighbours,
        localization,
    )
    dma = pltpu.SemaphoreType.DMA
    return pl.pallas_call(
        functools.partial(kernel, tiles, lags),
        out_shape=jax.ShapeDtypeStruct(prior.shape, BF16),
        in_specs=[SMEM] + [ANY] * len(args),
        out_specs=VMEM,
        scratch_shapes=[pltpu.VMEM(x.shape, x.dtype) for x in args]
        + [
            pltpu.VMEM((species, members, cols), BF16),
            pltpu.VMEM((rows * cols, 2 * members), F32),
            block,
            block,
            block,
            block,
            pltpu.VMEM((feats, slots), BF16),
            pltpu.VMEM((2, feats, halo), BF16),
            pltpu.VMEM((2, feats, halo), BF16),
            pltpu.VMEM((cols, slots), BF16),
            pltpu.VMEM((2, slots, halo), BF16),
            pltpu.VMEM((share // PACK, 2 * halo, PACK * members), BF16),
            pltpu.VMEM((cols, 2 * near), F32),
            pltpu.VMEM((cols, 2 * near), F32),
            dma((len(args),)),
            dma((lags - 1,)),
            dma,
            dma((lags - 1,)),
            dma((lags - 1,)),
            dma((2,)),
            dma((2,)),
            dma((lags - 1,)),
            dma((lags - 1,)),
            dma((3,)),
        ],
        compiler_params=pltpu.CompilerParams(collective_id=0, has_side_effects=True),
        name="smoother",
    )(obs_count, *args)


def solution(mesh):
    return jax.shard_map(
        body,
        mesh=mesh,
        in_specs=(
            P("lag", None, None, "space"),
            P("space"),
            P("space"),
            P(None, "space"),
            P("space"),
            P("space"),
            P(None, "space"),
            P(None, "space"),
            P(None, "space"),
        ),
        out_specs=P("lag", None, None, "space"),
        check_vma=False,
    )
```

time: 142 us -> 22.1 us (0.16)
  the two profiles are of different devices: /device:TPU:0 before, /device:TPU:21 now
where the time goes in v2:
time: 22.1 us; the launch traced here: 21.9 us
  Pallas kernels  19.7 us (89%)
  local copies, waits for them, and re-layouts  1.57 us (7%)
  between operations  0.66 us (3%)
    pallas_call x1, Pallas kernels, body(): pl.pallas_call(functools.partial(kernel, tiles, lags), out_shape=jax.Shap...  19.7 us
    unnamed x1, local copies, waits for them, and re-layouts  1.57 us

profile of v2, /device:TPU:21, one launch (start us, length us, event | category | flops | bytes accessed | tf_op | source)
XLA Modules:
  0.0 21.9 jit_solution(17621797479785515334)
XLA Ops:
  0.7 19.7 %smoother.1 = bf16[2,4,64,128]{3,2,1,0:T(8,128)(2,1)} custom-call(s32[1]{0:T(128)S(6)} %copy.11.count_ref, bf16[2,4,64,128]{3,2,1,0:T(8,128)(2,1)} %prior_ref.1, f32[1,1024]{1,0:T(1,128)} %bitcast.3, f32[1,1024]{1,0:T(1,128)} %bitcast.4, f32[4,1024]{1,0:T(4,128)} %coef_ref.1, s32[1,1024]{1,0:T(1,128)} %bitcast.5, s32[2,512]{1,0:T(2,128)} %lists_ref.1, ...), custom_call_target="tpu_custom_call" | custom-call | tf_op jit(solution)/shard_map/smoother/pallas_call | solution.py:360
  20.4 1.6 %copy.12 = bf16[2,4,64,128]{3,2,1,0:T(8,128)(2,1)} copy(bf16[2,4,64,128]{3,2,1,0:T(8,128)(2,1)} %smoother.1) | data formatting | bytes 262144

commit v3 on v2

--- a/solution.py
+++ b/solution.py
@@ -69,6 +69,9 @@
     feat_v,
     listed,
     around,
+    spread_mean,
+    spread_pert,
+    count_v,
     pick_v,
     list_v,
     near_v,
@@ -81,6 +84,9 @@
     swap_recv,
     halo_send,
     halo_recv,
+    pass_send,
+    pass_recv,
+    count_sem,
     back_send,
     back_recv,
     self_sem,
@@ -89,7 +95,10 @@
     windows, species, members, cols = prior_v.shape
     rows = windows * species
     share = cols // lags
-    slots, halo = column_v.shape[1], lists_v.shape[1]
+    slots, half = column_v.shape[1], lists_v.shape[1]
+    halo = 2 * half
+    core = lax.rem(me, 2)
+    partner = me + 1 - 2 * core
     near = table_v.shape[0]
     holder = lags - 1
     below, above = t > 0, t < tiles - 1
@@ -111,7 +120,7 @@
     pairs = [
         (prior_ref, prior_v),
         (column_ref, column_v),
-        (lists_ref, lists_v),
+        (lists_ref.at[:, pl.ds(pl.multiple_of(core * half, half), half)], lists_v),
         (coef_ref, coef_v),
         (value_ref, value_v),
         (weight_ref, weight_v),
@@ -119,6 +128,7 @@
         (local_ref, local_v),
     ]
     loads = [pltpu.make_async_copy(src, dst, in_sem.at[i]) for i, (src, dst) in enumerate(pairs)]
+    loads.append(pltpu.make_async_copy(count_ref, count_v, count_sem))
     for load in loads:
         load.start()
 
@@ -170,7 +180,7 @@
     for s in range(1, species):
         hx = hx + coef_v[s : s + 1, :] * dot(newest[s], pick)
     mean = jnp.sum(hx, axis=0, keepdims=True) / members
-    valid = jnp.where(iota((1, slots), 1) < count_ref[0], 1.0, 0.0)
+    valid = jnp.where(iota((1, slots), 1) < count_v[0], 1.0, 0.0)
     feat_v[:members] = ((hx - mean) * valid).astype(BF16)
     extra = feat_v.shape[0] - members
     row = iota((extra, slots), 0)
@@ -182,7 +192,11 @@
         listed[r] = dot(feat, list_v[r]).astype(BF16)
 
     def move(r, to):
-        return remote(listed.at[r], around.at[r], halo_send.at[r], halo_recv.at[r], {"space": to})
+        return remote(listed.at[r], around.at[r, core], halo_send.at[r], halo_recv.at[r], {"space": to})
+
+    def hand(r):
+        half_ref = around.at[r, core]
+        return remote(half_ref, half_ref, pass_send.at[r], pass_recv.at[r], {"lag": partner})
 
     @pl.when(above)
     def _():
@@ -241,29 +255,45 @@
         inner.append(dot(feat, onehot(table, slots)))
         near_v[q] = onehot(table - slots, 2 * halo)
 
+    for copy in swaps:
+        copy.wait()
+    mine.wait()
+    for q in qs:
+        at = slice(q * wide, (q + 1) * wide)
+        values = jnp.concatenate([got[l, :, at].astype(F32) for l in range(lags)], axis=0)
+        mean = dot(values.astype(BF16), ones) / members
+        spread_mean[:, at] = mean
+        spread_pert[:, at] = (values - mean).astype(BF16)
+
     @pl.when(above)
     def _():
+        move(1, up).wait_recv()
+        hand(1).start()
+
+    @pl.when(below)
+    def _():
+        move(0, down).wait_recv()
+        hand(0).start()
+
+    def part(q, h):
+        y = None
+        for r in range(2):
+            rows_at = pl.ds(pl.multiple_of((2 * r + h) * half, half), half)
+            term = dot(around[r, h], near_v[q, rows_at])
+            y = term if y is None else y + term
+        return y
+
+    inner = [inner[q] + part(q, core) for q in qs]
+
+    @pl.when(above)
+    def _():
         move(0, up).wait_send()
-        move(1, up).wait_recv()
+        hand(1).wait()
 
     @pl.when(below)
     def _():
         move(1, down).wait_send()
-        move(0, down).wait_recv()
-
-    picked = [
-        inner[q] + dot(around[0], near_v[q, :halo]) + dot(around[1], near_v[q, halo:]) for q in qs
-    ]
-    gathered = [picked[q][:members] for q in qs]
-    weighted = [(gathered[q] * (local[q] * picked[q][members : members + 1])).astype(BF16) for q in qs]
-    gram = [
-        lax.dot_general(
-            gathered[q].astype(BF16), diag(weighted[q]), (((1,), (1,)), ((), ())), preferred_element_type=F32
-        )
-        for q in qs
-    ]
-    matrix = [eye + gram[q] / (members - 1) for q in qs]
-    total = [jnp.sum(matrix[q] * matrix[q], axis=0, keepdims=True) for q in qs]
+        hand(0).wait()
 
     def group_sum(x):
         high, _ = split(x)
@@ -272,51 +302,65 @@
         y = dot(jnp.concatenate([high.astype(F32), mid.astype(F32), last.astype(F32)], axis=0).astype(BF16), ones)
         return y[:count] + y[count : 2 * count] + y[2 * count :]
 
-    root = lax.rsqrt(group_sum(jnp.concatenate(total, axis=0)))
-    inv = [root[q : q + 1] for q in qs]
-    a = [matrix[q] * inv[q] for q in qs]
-    ab = [a[q].astype(BF16) for q in qs]
-    p = [dot(ab[q], diag(ab[q])) for q in qs]
-    z = [
-        2.25 * eye
-        - 2.4375 * a[q]
-        + 1.6875 * p[q]
-        + dot((0.0625 * p[q] - 0.5625 * a[q]).astype(BF16), diag(p[q].astype(BF16)))
-        for q in qs
-    ]
-    zs = [jnp.concatenate(split(z[q]), axis=0) for q in qs]
-
-    def apply(q, x):
-        high, small = split(x)
-        y = dot(zs[q], diag(high))
-        return y[:members] + y[members:] + dot(zs[q][:members], diag(small))
-
-    drive = []
-    for q in qs:
-        x = weighted[q].astype(F32) * picked[q][members + 1 : members + 2]
-        y = dot(jnp.concatenate(split(x), axis=0), ones)
-        drive.append(y[:members] + y[members:])
-    u = [apply(q, drive[q]) for q in qs]
-    mean_weight = [apply(q, u[q]) for q in qs]
-    trans = [
-        (z[q] * jnp.sqrt(inv[q]) + mean_weight[q] * (inv[q] / (members - 1))).astype(BF16) for q in qs
-    ]
-
-    for copy in swaps:
-        copy.wait()
-    mine.wait()
-    for q in qs:
-        prior = jnp.concatenate([got[l, :, q * wide : (q + 1) * wide].astype(F32) for l in range(lags)], axis=0)
-        mean = dot(prior.astype(BF16), ones) / members
-        mixed = mean + dot((prior - mean).astype(BF16), diag(trans[q]))
-        for l in range(lags):
-            back[l, :, q * wide : (q + 1) * wide] = mixed[l * rows : (l + 1) * rows].astype(BF16)
-    returns = [
-        remote(back.at[peer], home.at[me], back_send.at[d], back_recv.at[d], {"lag": peer})
-        for d, peer in enumerate(peers)
-    ]
-    for copy in returns:
-        copy.start()
+    def solve(qs):
+        picked = {q: inner[q] + part(q, 1 - core) for q in qs}
+        gathered = {q: picked[q][:members] for q in qs}
+        weighted = {q: (gathered[q] * (local[q] * picked[q][members : members + 1])).astype(BF16) for q in qs}
+        gram = {
+            q: lax.dot_general(
+                gathered[q].astype(BF16), diag(weighted[q]), (((1,), (1,)), ((), ())), preferred_element_type=F32
+            )
+            for q in qs
+        }
+        matrix = {q: eye + gram[q] / (members - 1) for q in qs}
+        total = [jnp.sum(matrix[q] * matrix[q], axis=0, keepdims=True) for q in qs]
+        root = lax.rsqrt(group_sum(jnp.concatenate(total, axis=0)))
+        inv = {q: root[i : i + 1] for i, q in enumerate(qs)}
+        a = {q: matrix[q] * inv[q] for q in qs}
+        ab = {q: a[q].astype(BF16) for q in qs}
+        p = {q: dot(ab[q], diag(ab[q])) for q in qs}
+        z = {
+            q: 2.25 * eye
+            - 2.4375 * a[q]
+            + 1.6875 * p[q]
+            + dot((0.0625 * p[q] - 0.5625 * a[q]).astype(BF16), diag(p[q].astype(BF16)))
+            for q in qs
+        }
+        zs = {q: jnp.concatenate(split(z[q]), axis=0) for q in qs}
+
+        def apply(q, x):
+            high, small = split(x)
+            y = dot(zs[q], diag(high))
+            return y[:members] + y[members:] + dot(zs[q][:members], diag(small))
+
+        drive = {}
+        for q in qs:
+            x = weighted[q].astype(F32) * picked[q][members + 1 : members + 2]
+            y = dot(jnp.concatenate(split(x), axis=0), ones)
+            drive[q] = y[:members] + y[members:]
+        u = {q: apply(q, drive[q]) for q in qs}
+        mean_weight = {q: apply(q, u[q]) for q in qs}
+        for q in qs:
+            trans = (z[q] * jnp.sqrt(inv[q]) + mean_weight[q] * (inv[q] / (members - 1))).astype(BF16)
+            at = slice(q * wide, (q + 1) * wide)
+            mixed = spread_mean[:, at] + dot(spread_pert[:, at], diag(trans))
+            for l in range(lags):
+                back[l, :, at] = mixed[l * rows : (l + 1) * rows].astype(BF16)
+
+    returns = []
+    batch = -(-groups // 2)
+    for b in range(2):
+        first, last = b * batch, min(groups, (b + 1) * batch)
+        if first >= last:
+            continue
+        solve(range(first, last))
+        lanes = pl.ds(first * wide, (last - first) * wide)
+        for d, peer in enumerate(peers):
+            copy = remote(
+                back.at[peer, :, lanes], home.at[me, :, lanes], back_send.at[b, d], back_recv.at[b, d], {"lag": peer}
+            )
+            copy.start()
+            returns.append(copy)
     mine = pltpu.make_async_copy(back.at[me], home.at[me], self_sem.at[2])
     mine.start()
 
@@ -345,7 +389,7 @@
     share = cols // lags
     rows = windows * species
     block = pltpu.VMEM((lags, rows, share * members), BF16)
-    feats = members + 16
+    feats = members + 8
     args = (
         prior,
         obs_value.reshape(1, slots),
@@ -360,9 +404,11 @@
     return pl.pallas_call(
         functools.partial(kernel, tiles, lags),
         out_shape=jax.ShapeDtypeStruct(prior.shape, BF16),
-        in_specs=[SMEM] + [ANY] * len(args),
+        in_specs=[ANY] * (1 + len(args)),
         out_specs=VMEM,
-        scratch_shapes=[pltpu.VMEM(x.shape, x.dtype) for x in args]
+        scratch_shapes=[
+            pltpu.VMEM((2, halo // 2) if x is halo_lists else x.shape, x.dtype) for x in args
+        ]
         + [
             pltpu.VMEM((species, members, cols), BF16),
             pltpu.VMEM((rows * cols, 2 * members), F32),
@@ -371,10 +417,13 @@
             block,
             block,
             pltpu.VMEM((feats, slots), BF16),
-            pltpu.VMEM((2, feats, halo), BF16),
-            pltpu.VMEM((2, feats, halo), BF16),
+            pltpu.VMEM((2, feats, halo // 2), BF16),
+            pltpu.VMEM((2, 2, feats, halo // 2), BF16),
+            pltpu.VMEM((lags * rows, share * members), F32),
+            pltpu.VMEM((lags * rows, share * members), BF16),
+            pltpu.SMEM((1,), jnp.int32),
             pltpu.VMEM((cols, slots), BF16),
-            pltpu.VMEM((2, slots, halo), BF16),
+            pltpu.VMEM((2, slots, halo // 2), BF16),
             pltpu.VMEM((share // PACK, 2 * halo, PACK * members), BF16),
             pltpu.VMEM((cols, 2 * near), F32),
             pltpu.VMEM((cols, 2 * near), F32),
@@ -385,8 +434,11 @@
             dma((lags - 1,)),
             dma((2,)),
             dma((2,)),
-            dma((lags - 1,)),
-            dma((lags - 1,)),
+            dma((2,)),
+            dma((2,)),
+            dma,
+            dma((2, lags - 1)),
+            dma((2, lags - 1)),
             dma((3,)),
         ],
         compiler_params=pltpu.CompilerParams(collective_id=0, has_side_effects=True),

time: 22.1 us -> 21.4 us (0.968)
  the two profiles are of different devices: /device:TPU:21 before, /device:TPU:0 now
where the time goes in v3:
time: 21.4 us; the launch traced here: 21.2 us
  Pallas kernels  19 us (89%)
  local copies, waits for them, and re-layouts  1.57 us (7%)
  between operations  0.66 us (3%)
    pallas_call x1, Pallas kernels, body(): pl.pallas_call(functools.partial(kernel, tiles, lags), out_shape=jax.Shap...  19 us
    unnamed x1, local copies, waits for them, and re-layouts  1.57 us

profile of v3, /device:TPU:0, one launch (start us, length us, event | category | flops | bytes accessed | tf_op | source)
XLA Modules:
  0.0 21.2 jit_solution(608024628789335126)
XLA Ops:
  0.7 19.0 %smoother.1 = bf16[2,4,64,128]{3,2,1,0:T(8,128)(2,1)} custom-call(s32[1]{0:T(128)S(6)} %copy.11.count_ref, bf16[2,4,64,128]{3,2,1,0:T(8,128)(2,1)} %prior_ref.1, f32[1,1024]{1,0:T(1,128)} %bitcast.3, f32[1,1024]{1,0:T(1,128)} %bitcast.4, f32[4,1024]{1,0:T(4,128)} %coef_ref.1, s32[1,1024]{1,0:T(1,128)} %bitcast.5, s32[2,512]{1,0:T(2,128)} %lists_ref.1, ...), custom_call_target="tpu_custom_call" | custom-call | tf_op jit(solution)/shard_map/smoother/pallas_call | solution.py:404
  19.7 1.6 %copy.12 = bf16[2,4,64,128]{3,2,1,0:T(8,128)(2,1)} copy(bf16[2,4,64,128]{3,2,1,0:T(8,128)(2,1)} %smoother.1) | data formatting | bytes 262144

commit v4 on v3

--- a/solution.py
+++ b/solution.py
@@ -51,7 +51,7 @@
     lists_ref,
     table_ref,
     local_ref,
-    out_ref,
+    home,
     prior_v,
     value_v,
     weight_v,
@@ -65,7 +65,6 @@
     send,
     got,
     back,
-    home,
     feat_v,
     listed,
     around,
@@ -372,9 +371,15 @@
     mine.wait()
     for copy in returns:
         copy.wait()
+
+
+def restore_kernel(got_ref, out_ref, turned):
+    windows, species, members, cols = out_ref.shape
+    rows = windows * species
+    share = cols // got_ref.shape[0]
     for c in range(0, cols, 2):
         at = (c % share) * members
-        x = home[c // share, :, at : at + 2 * members].astype(F32)
+        x = got_ref[c // share, :, at : at + 2 * members].astype(F32)
         turned[pl.ds(c, rows, stride=cols), :] = x
         turned[pl.ds(c + 1, rows, stride=cols), :] = pltpu.roll(x, members, 1)
     for r in range(rows):
@@ -401,18 +406,17 @@
         localization,
     )
     dma = pltpu.SemaphoreType.DMA
-    return pl.pallas_call(
+    home = pl.pallas_call(
         functools.partial(kernel, tiles, lags),
-        out_shape=jax.ShapeDtypeStruct(prior.shape, BF16),
+        out_shape=jax.ShapeDtypeStruct((lags, rows, share * members), BF16),
         in_specs=[ANY] * (1 + len(args)),
-        out_specs=VMEM,
+        out_specs=ANY,
         scratch_shapes=[
             pltpu.VMEM((2, halo // 2) if x is halo_lists else x.shape, x.dtype) for x in args
         ]
         + [
             pltpu.VMEM((species, members, cols), BF16),
             pltpu.VMEM((rows * cols, 2 * members), F32),
-            block,
             block,
             block,
             block,
@@ -444,6 +448,14 @@
         compiler_params=pltpu.CompilerParams(collective_id=0, has_side_effects=True),
         name="smoother",
     )(obs_count, *args)
+    return pl.pallas_call(
+        restore_kernel,
+        out_shape=jax.ShapeDtypeStruct(prior.shape, BF16),
+        in_specs=[VMEM],
+        out_specs=VMEM,
+        scratch_shapes=[pltpu.VMEM((rows * cols, 2 * members), F32)],
+        name="restore",
+    )(home)
 
 
 def solution(mesh):

time: 21.4 us -> 20.8 us (0.972)
  local copies, waits for them, and re-layouts: 1.57 us -> 0 us
  Pallas kernels: 19 us -> 20 us
    pallas_call x0 -> x1, Pallas kernels: none -> 1.97 us  [body(): pl.pallas_call(restore_kernel, out_shape=jax.ShapeDtypeStruct(prior.shape...]
    unnamed x1 -> x0, local copies, waits for them, and re-layouts: 1.57 us -> none
    pallas_call x1, Pallas kernels: 19 us -> 18.1 us  [body(): pl.pallas_call(functools.partial(kernel, tiles, lags), out_shape=jax.Shap...]
where the time goes in v4:
time: 20.8 us; the launch traced here: 20.7 us
  Pallas kernels  20 us (96%)
  between operations  0.66 us (3%)
    pallas_call x1, Pallas kernels, body(): pl.pallas_call(functools.partial(kernel, tiles, lags), out_shape=jax.Shap...  18.1 us
    pallas_call x1, Pallas kernels, body(): pl.pallas_call(restore_kernel, out_shape=jax.ShapeDtypeStruct(prior.shape...  1.97 us

profile of v4, /device:TPU:0, one launch (start us, length us, event | category | flops | bytes accessed | tf_op | source)
XLA Modules:
  0.0 20.7 jit_solution(16337149078117015919)
XLA Ops:
  0.7 18.1 %smoother.1.got_ref = bf16[4,8,2048]{2,1,0:T(8,128)(2,1)} custom-call(s32[1]{0:T(128)S(6)} %copy.10.count_ref, bf16[2,4,64,128]{3,2,1,0:T(8,128)(2,1)} %prior_ref.1, f32[1,1024]{1,0:T(1,128)} %bitcast.3, f32[1,1024]{1,0:T(1,128)} %bitcast.4, f32[4,1024]{1,0:T(4,128)} %coef_ref.1, s32[1,1024]{1,0:T(1,128)} %bitcast.5, s32[2,512]{1,0:T(2,128)} %lists_ref.1, ...), custom_call_target="tpu_custom_call" | custom-call | tf_op jit(solution)/shard_map/smoother/pallas_call | solution.py:409
  18.7 2.0 %restore.1 = bf16[2,4,64,128]{3,2,1,0:T(8,128)(2,1)} custom-call(bf16[4,8,2048]{2,1,0:T(8,128)(2,1)} %smoother.1.got_ref), custom_call_target="tpu_custom_call" | custom-call | tf_op jit(solution)/shard_map/restore/pallas_call | solution.py:451
